TPU v7x, 32 devices: a whole 2x2x4 slice. The times are simulated.
32 devices in a mesh: fsdp: 8 (over z, y), ep: 4 (over x, core).
Axes of the slice: x: 2, y: 2, z: 4, core: 2. Of those that a mesh axis runs over, the one named last changes fastest.
Arguments:
- tokens: bfloat16 [4096, 3072], P(('fsdp', 'ep')), may hold values from -6 to 6
- expert_ids: int32 [4096, 2], P(('fsdp', 'ep')), may hold values from 0 to 3, all different within a row; in each aligned block of 128 rows (0 to 127, 128 to 255, ...) at most 128 rows name the same one
- gates: float32 [4096, 2], P(('fsdp', 'ep')), may hold values from 0.2 to 1
- up_weight: bfloat16 [4, 3072, 768], P('ep', 'fsdp'), may hold values from -0.109375 to 0.109375
- down_weight: bfloat16 [4, 768, 3072], P('ep', 'fsdp'), may hold values from -0.21875 to 0.21875
- cotangent: bfloat16 [4096, 3072], P(('fsdp', 'ep')), may hold values from -6 to 6
Outputs:
- mixed: bfloat16 [4096, 3072], P(('fsdp', 'ep'))
- token_grad: bfloat16 [4096, 3072], P(('fsdp', 'ep'))
- up_grad: bfloat16 [4, 3072, 768], P('ep', 'fsdp')
- down_grad: bfloat16 [4, 768, 3072], P('ep', 'fsdp')
Inputs may be any that keep to these rules, and one draw needn't show every extreme that they name: `expert_ids`: each token names two different experts. Among the tokens of one device (aligned blocks of 128 tokens) no expert is named more than 128 times, and in some block one expert is named exactly 128 times.
All inputs are finite; a program needn't handle non-finite values.
Results may differ from a plain program's by a relative error of at most 0.012.
Values may be sent and summed in bfloat16 or wider, within the bound.
A program may use at most 128 MiB of HBM per device.

v0:
```python
import jax
import jax.numpy as jnp
from jax import lax
from jax.sharding import PartitionSpec as P


def gelu_parts(pre):
    root = 0.7978845608028654
    inner = root * (pre + 0.044715 * pre * pre * pre)
    tanh_val = jnp.tanh(inner)
    value = 0.5 * pre * (1.0 + tanh_val)
    slope = 0.5 * (1.0 + tanh_val) + 0.5 * pre * (1.0 - tanh_val * tanh_val) * root * (
        1.0 + 3.0 * 0.044715 * pre * pre
    )
    return (value, slope)


def contract_last(left, right):
    return lax.dot_general(
        left, right, (((1,), (1,)), ((), ())), preferred_element_type=jnp.float32
    )


def contract_first(left, right):
    return lax.dot_general(
        left, right, (((0,), (0,)), ((), ())), preferred_element_type=jnp.float32
    )


def body(tokens, expert_ids, gates, up_weight, down_weight, cotangent):
    n_ep = lax.axis_size("ep")
    f32 = jnp.float32
    bf16 = jnp.bfloat16
    chosen = expert_ids[:, :, None] == jnp.arange(n_ep, dtype=jnp.int32)[None, None, :]
    dense_gates = jnp.sum(jnp.where(chosen, gates[:, :, None], 0.0), axis=1)
    all_gates = lax.all_gather(dense_gates, "ep", axis=0, tiled=True)
    mine = lax.axis_index("ep") == jnp.arange(n_ep, dtype=jnp.int32)
    gate = jnp.sum(jnp.where(mine[None, :], all_gates, 0.0), axis=1, keepdims=True)
    rows = lax.all_gather(tokens, "ep", axis=0, tiled=True)
    up = lax.all_gather(up_weight, "fsdp", axis=1, tiled=True)[0]
    cot = lax.all_gather(cotangent, "ep", axis=0, tiled=True)
    down = lax.all_gather(down_weight, "fsdp", axis=1, tiled=True)[0]
    grad_rows = (cot.astype(f32) * gate).astype(bf16)
    pre = jnp.dot(rows, up, preferred_element_type=f32)
    value, slope = gelu_parts(pre)
    hidden = value.astype(bf16)
    down_grad = lax.psum_scatter(
        contract_first(hidden, grad_rows).astype(bf16), "fsdp", scatter_dimension=0, tiled=True
    )
    d_hidden = contract_last(grad_rows, down)
    d_pre = (d_hidden * slope).astype(bf16)
    up_grad = lax.psum_scatter(
        contract_first(rows, d_pre).astype(bf16), "fsdp", scatter_dimension=0, tiled=True
    )
    result = jnp.dot(hidden, down, preferred_element_type=f32)
    mixed = lax.psum_scatter((result * gate).astype(bf16), "ep", scatter_dimension=0, tiled=True)
    back = contract_last(d_pre, up).astype(bf16)
    token_grad = lax.psum_scatter(back, "ep", scatter_dimension=0, tiled=True)
    return (mixed, token_grad, up_grad[None], down_grad[None])


def solution(mesh):
    placed = (
        P(("fsdp", "ep"), None),
        P(("fsdp", "ep"), None),
        P(("fsdp", "ep"), None),
        P("ep", "fsdp", None),
        P("ep", "fsdp", None),
        P(("fsdp", "ep"), None),
    )
    return jax.shard_map(
        body,
        mesh=mesh,
        in_specs=placed,
        out_specs=(
            P(("fsdp", "ep"), None),
            P(("fsdp", "ep"), None),
            P("ep", "fsdp", None),
            P("ep", "fsdp", None),
        ),
        check_vma=False,
    )
```

profile of v0, /device:TPU:0, one launch (start us, length us, event | category | flops | bytes accessed | tf_op | source)
XLA Modules:
  0.0 534.1 jit_solution(15591842795536665031)
XLA Ops:
  7.2 0.7 all-gather.5.cloned.1.call-update
  8.0 0.7 all-gather.7.cloned.1.call-update
  10.1 6.1 %all_gather.18 = f32[512,4]{0,1:T(4,128)S(1)} all-gather(f32[128,4]{0,1:T(4,128)S(1)} %select_reduce_fusion.1), channel_id=1, replica_groups=mesh['fsdp'=8,'ep'=4] {'ep'}, dimensions={0}, use_global_device_ids=true | all-gather | bytes 10240 | tf_op jit(solution)/shard_map/all_gather | solution.py:36
  16.3 24.6 %all-gather.5.cloned.1.call-done = bf16[512,3072]{1,0:T(8,128)(2,1)} async-done(((bf16[128,3072]{1,0:T(8,128)(2,1)}), bf16[512,3072]{1,0:T(8,128)(2,1)}) %all-gather.5.cloned.1.call-update) | async-done | bytes 3145744 | tf_op jit(solution)/shard_map/all_gather | solution.py:39
  40.8 82.1 %all-gather.7.cloned.1.call-done = bf16[1,3072,768]{2,1,0:T(8,128)(2,1)} async-done(((bf16[1,384,768]{2,1,0:T(8,128)(2,1)}), bf16[1,3072,768]{2,1,0:T(8,128)(2,1)}) %all-gather.7.cloned.1.call-update) | async-done | bytes 4718608 | tf_op jit(solution)/shard_map/all_gather | solution.py:40
  122.9 7.1 %fusion.5 = f32[512,768]{1,0:T(8,128)} fusion(bf16[512,3072]{1,0:T(8,128)(2,1)} %all-gather.5.cloned.1.call-done, bf16[1,3072,768]{2,1,0:T(8,128)(2,1)} %all-gather.7.cloned.1.call-done), kind=kOutput, calls=%fused_computation.9 | convolution fusion | flops 2415919104 | bytes 9437184 | tf_op jit(solution)/shard_map/dot_general | solution.py:44
  130.0 21.2 %all-gather.11.cloned.1.call-done = bf16[512,3072]{1,0:T(8,128)(2,1)} async-done(((bf16[128,3072]{1,0:T(8,128)(2,1)}), bf16[512,3072]{1,0:T(8,128)(2,1)}) %all-gather.11.cloned.1.call-update) | async-done | bytes 3145744 | tf_op jit(solution)/shard_map/all_gather | solution.py:41
  151.2 82.0 %all-gather.9.cloned.1.call-done = bf16[1,768,3072]{2,1,0:T(8,128)(2,1)} async-done(((bf16[1,96,3072]{2,1,0:T(8,128)(2,1)}), bf16[1,768,3072]{2,1,0:T(8,128)(2,1)}) %all-gather.9.cloned.1.call-update) | async-done | bytes 4718608 | tf_op jit(solution)/shard_map/all_gather | solution.py:42
  233.2 7.0 %fusion.17 = bf16[512,768]{1,0:T(8,128)(2,1)S(1)} fusion(f32[512,768]{1,0:T(8,128)} %fusion.5, bf16[1,768,3072]{2,1,0:T(8,128)(2,1)} %all-gather.9.cloned.1.call-done, bf16[512,3072]{1,0:T(8,128)(2,1)} %all-gather.11.cloned.1.call-done, f32[512]{0:T(512)S(1)} %select_reduce_fusion), kind=kOutput, calls=%fused_computation.21 | convolution fusion | flops 2428108800 | bytes 10225664 | tf_op jit(solution)/shard_map/dot_general | solution.py:19
  240.2 0.9 copy-done.5
  241.1 4.3 fusion.7
  245.4 6.7 %copy.17 = bf16[3072,768]{1,0:T(8,128)(2,1)} copy(bf16[3072,768]{0,1:T(8,128)(2,1)} %fusion.7) | data formatting | bytes 9437184
  252.2 1.3 copy-done.4
  253.6 6.5 %multiply_convert_fusion.1 = bf16[512,3072]{1,0:T(8,128)(2,1)} fusion(bf16[1,768,3072]{2,1,0:T(8,128)(2,1)} %all-gather.9.cloned.1.call-done, f32[512]{0:T(512)S(1)} %select_reduce_fusion, f32[512,768]{1,0:T(8,128)S(1)} %copy-done.4), kind=kOutput, calls=%fused_computation.1 | convolution fusion | flops 2422603776 | bytes 9439232 | tf_op jit(solution)/shard_map/dot_general | solution.py:55
  260.1 1.1 copy-done.6
  261.1 6.4 %fusion.8 = bf16[512,3072]{1,0:T(8,128)(2,1)} fusion(bf16[512,768]{1,0:T(8,128)(2,1)S(1)} %copy-done.6, bf16[1,3072,768]{2,1,0:T(8,128)(2,1)} %all-gather.7.cloned.1.call-done), kind=kOutput, calls=%fused_computation.12 | convolution fusion | flops 2417491968 | bytes 8650752 | tf_op jit(solution)/shard_map/dot_general | solution.py:19
  267.6 1.8 copy-done.2
  269.5 6.5 %convolution_convert_fusion = bf16[768,3072]{1,0:T(8,128)(2,1)} fusion(bf16[512,3072]{1,0:T(8,128)(2,1)S(1)} %copy-done.2, f32[512]{0:T(512)S(1)} %select_reduce_fusion, f32[512,768]{1,0:T(8,128)} %fusion.5), kind=kOutput, calls=%fused_computation.2 | convolution fusion | flops 2426535936 | bytes 9439232 | tf_op jit(solution)/shard_map/dot_general | solution.py:25
  276.0 69.8 %reduce-scatter.13.cloned.1.call-done = bf16[384,768]{1,0:T(8,128)(2,1)} async-done(((bf16[3072,768]{1,0:T(8,128)(2,1)}), bf16[384,768]{1,0:T(8,128)(2,1)}) %reduce-scatter.13.cloned.1.call-update) | async-done | bytes 589840
  345.7 1.4 copy.18
  347.1 1.1 copy.16
  348.2 38.3 %reduce-scatter.7.cloned.1.call-done = bf16[128,3072]{1,0:T(8,128)(2,1)} async-done(((bf16[512,3072]{1,0:T(8,128)(2,1)}), bf16[128,3072]{1,0:T(8,128)(2,1)}) %reduce-scatter.7.cloned.1.call-update) | async-done | bytes 786448 | tf_op jit(solution)/shard_map/reduce_scatter | solution.py:56
  386.4 41.2 %reduce-scatter.9.cloned.1.call-done = bf16[128,3072]{1,0:T(8,128)(2,1)} async-done(((bf16[512,3072]{1,0:T(8,128)(2,1)}), bf16[128,3072]{1,0:T(8,128)(2,1)}) %reduce-scatter.9.cloned.1.call-update) | async-done | bytes 786448 | tf_op jit(solution)/shard_map/reduce_scatter | solution.py:58
  427.6 99.7 %reduce-scatter.11.cloned.1.call-done = bf16[96,3072]{1,0:T(8,128)(2,1)} async-done(((bf16[768,3072]{1,0:T(8,128)(2,1)}), bf16[96,3072]{1,0:T(8,128)(2,1)}) %reduce-scatter.11.cloned.1.call-update) | async-done | bytes 589840 | tf_op jit(solution)/shard_map/reduce_scatter | solution.py:47
  (27 shorter events, 1.7 us)
Async XLA Ops:
  7.2 2.9 copy-start
  7.2 2.9 copy-start.1
  7.2 33.7 %all-gather.5.cloned.1.call-start = ((), (), s32[]{:S(2)}) async-start(), calls=%async_computation.4 | async-start | bytes 3932160 | tf_op jit(solution)/shard_map/all_gather | solution.py:39
  7.9 115.0 %all-gather.7.cloned.1.call-start = ((), (), s32[]{:S(2)}) async-start(), calls=%async_computation.5 | async-start | bytes 5308416 | tf_op jit(solution)/shard_map/all_gather | solution.py:40
  8.7 142.5 %all-gather.11.cloned.1.call-start = ((), (), s32[]{:S(2)}) async-start(), calls=%async_computation.8 | async-start | bytes 3932160 | tf_op jit(solution)/shard_map/all_gather | solution.py:41
  9.4 223.8 %all-gather.9.cloned.1.call-start = ((), (), s32[]{:S(2)}) async-start(), calls=%async_computation.6 | async-start | bytes 5308416 | tf_op jit(solution)/shard_map/all_gather | solution.py:42
  10.0 335.7 %reduce-scatter.13.cloned.1.call-start = ((), (), s32[]{:S(2)}) async-start(), calls=%async_computation.11 | async-start | bytes 5308416
  130.0 111.0 %copy-start.3 = (bf16[512,3072]{1,0:T(8,128)(2,1)S(1)}, bf16[512,3072]{1,0:T(8,128)(2,1)}, u32[]{:S(2)}) copy-start(bf16[512,3072]{1,0:T(8,128)(2,1)} %all-gather.5.cloned.1.call-done) | copy-start | bytes 9437188
  240.2 0.9 copy-start.5
  252.1 1.4 copy-start.4
  252.2 134.2 %reduce-scatter.7.cloned.1.call-start = ((), (), s32[]{:S(2)}) async-start(), calls=%async_computation.7 | async-start | bytes 3932160 | tf_op jit(solution)/shard_map/reduce_scatter | solution.py:56
  260.0 1.1 copy-start.6
  260.0 167.6 %reduce-scatter.9.cloned.1.call-start = ((), (), s32[]{:S(2)}) async-start(), calls=%async_computation.9 | async-start | bytes 3932160 | tf_op jit(solution)/shard_map/reduce_scatter | solution.py:58
  267.5 1.9 copy-start.2
  267.6 259.7 %reduce-scatter.11.cloned.1.call-start = ((), (), s32[]{:S(2)}) async-start(), calls=%async_computation.10 | async-start | bytes 5308416 | tf_op jit(solution)/shard_map/reduce_scatter | solution.py:47
Sparse Core Ops, SparseCore 0:
  9.6 31.2 all-gather.4
  43.0 79.8 all-gather.6
  124.5 26.6 all-gather.10
  153.3 79.8 all-gather.8
  252.3 93.3 reduce-scatter.12
  348.7 37.6 reduce-scatter.6
  389.7 37.9 reduce-scatter.8
  431.9 95.3 reduce-scatter.10
where the time goes:
time: 535 us; the launch traced here: 534 us
  waiting for transfers between devices  461 us (86%)
  matrix products  37.8 us (7%)
  local copies, waits for them, and re-layouts  14.3 us (3%)
  between operations  14.2 us (3%)
  blocking collectives  6.11 us (1%)
    reduce_scatter x1, waiting for transfers between devices, body(): lax.psum_scatter(contract_first(hidden, grad_rows).astype(bf16), 'fsdp',...  99.7 us
    all_gather x1, waiting for transfers between devices, body(): up = lax.all_gather(up_weight, 'fsdp', axis=1, tiled=True)[0]  82.1 us
    all_gather x1, waiting for transfers between devices, body(): down = lax.all_gather(down_weight, 'fsdp', axis=1, tiled=True)[0]  82 us
    unnamed x9, waiting for transfers between devices  72.4 us
    reduce_scatter x1, waiting for transfers between devices, body(): token_grad = lax.psum_scatter(back, 'ep', scatter_dimension=0, tiled=True)  41.2 us
    reduce_scatter x1, waiting for transfers between devices, body(): lax.psum_scatter((result * gate).astype(bf16), 'ep', scatter_dimension=0,...  38.3 us
    all_gather x1, waiting for transfers between devices, body(): rows = lax.all_gather(tokens, 'ep', axis=0, tiled=True)  24.6 us
    all_gather x1, waiting for transfers between devices, body(): cot = lax.all_gather(cotangent, 'ep', axis=0, tiled=True)  21.2 us
  transfers between devices with their start and end apart: 8, of which 8 were waited for; matrix products, arithmetic and copies ran while one was open for 5% of the time, Pallas kernels for 0%

commit v1 on v0

--- a/solution.py
+++ b/solution.py
@@ -1,7 +1,25 @@
+import functools
 import jax
 import jax.numpy as jnp
 from jax import lax
 from jax.sharding import PartitionSpec as P
+
+
+def see_task(a0, mesh_ax):
+    nd = lax.axis_size(mesh_ax)
+    series = [(kk, (kk + 1) % nd) for kk in range(nd)]
+
+    def create_widths(last):
+        if len(last) == nd:
+            return last
+        return create_widths([lax.ppermute(last[0], mesh_ax, series), *last])
+
+    o_now = create_widths([a0])
+    g_now = jnp.concatenate(o_now, axis=0)
+    return jnp.roll(g_now, (lax.axis_index(mesh_ax) + 1) * a0.shape[0], axis=0)
+
+
+part_levels_all = functools.partial(see_task, mesh_ax="ep")
 
 
 def gelu_parts(pre):
@@ -36,7 +54,7 @@
     all_gates = lax.all_gather(dense_gates, "ep", axis=0, tiled=True)
     mine = lax.axis_index("ep") == jnp.arange(n_ep, dtype=jnp.int32)
     gate = jnp.sum(jnp.where(mine[None, :], all_gates, 0.0), axis=1, keepdims=True)
-    rows = lax.all_gather(tokens, "ep", axis=0, tiled=True)
+    rows = part_levels_all(tokens)
     up = lax.all_gather(up_weight, "fsdp", axis=1, tiled=True)[0]
     cot = lax.all_gather(cotangent, "ep", axis=0, tiled=True)
     down = lax.all_gather(down_weight, "fsdp", axis=1, tiled=True)[0]

time: 535 us -> 489 us (0.914)
  waiting for transfers between devices: 461 us -> 415 us
  local copies, waits for them, and re-layouts: 14.3 us -> 7.56 us
  blocking collectives: 6.11 us -> 11.5 us
    reduce_scatter x0 -> x1, waiting for transfers between devices: none -> 99.5 us  [body(): lax.psum_scatter(contract_first(rows, d_pre).astype(bf16), 'fsdp', scatte...]
    unnamed x9 -> x7, waiting for transfers between devices: 72.4 us -> 1.46 us
    all_gather x1, waiting for transfers between devices: 82.1 us -> 40.4 us  [body(): up = lax.all_gather(up_weight, 'fsdp', axis=1, tiled=True)[0]]
    reduce_scatter x1, waiting for transfers between devices: 38.3 us -> 13.5 us  [body(): lax.psum_scatter((result * gate).astype(bf16), 'ep', scatter_dimension=0,...]
    all_gather x1 -> x0, waiting for transfers between devices: 24.6 us -> none  [body(): rows = lax.all_gather(tokens, 'ep', axis=0, tiled=True)]
    ppermute x0 -> x3, waiting for transfers between devices: none -> 23.2 us  [create_widths(): return create_widths([lax.ppermute(last[0], mesh_ax, series), *last])]
    unnamed x17 -> x9, local copies, waits for them, and re-layouts: 14.3 us -> 6.61 us
    all_gather x1, waiting for transfers between devices: 82 us -> 74.3 us  [body(): down = lax.all_gather(down_weight, 'fsdp', axis=1, tiled=True)[0]]
  transfers between devices with their start and end apart: 8 -> 10, of which waited for: 8 -> 9; matrix products, arithmetic and copies ran while one was open for 5% -> 10% of each run, Pallas kernels for 0% -> 0%
where the time goes in v1:
time: 489 us
  waiting for transfers between devices  415 us (85%)
  matrix products  39.6 us (8%)
  between operations  14.2 us (3%)
  blocking collectives  11.5 us (2%)
  local copies, waits for them, and re-layouts  7.56 us (2%)
    reduce_scatter x1, waiting for transfers between devices, body(): lax.psum_scatter(contract_first(rows, d_pre).astype(bf16), 'fsdp', scatte...  99.5 us
    reduce_scatter x1, waiting for transfers between devices, body(): lax.psum_scatter(contract_first(hidden, grad_rows).astype(bf16), 'fsdp',...  99.3 us
    all_gather x1, waiting for transfers between devices, body(): down = lax.all_gather(down_weight, 'fsdp', axis=1, tiled=True)[0]  74.3 us
    reduce_scatter x1, waiting for transfers between devices, body(): token_grad = lax.psum_scatter(back, 'ep', scatter_dimension=0, tiled=True)  41.1 us
    all_gather x1, waiting for transfers between devices, body(): up = lax.all_gather(up_weight, 'fsdp', axis=1, tiled=True)[0]  40.4 us
    ppermute x3, waiting for transfers between devices, create_widths(): return create_widths([lax.ppermute(last[0], mesh_ax, series), *last])  23.2 us
    all_gather x1, waiting for transfers between devices, body(): cot = lax.all_gather(cotangent, 'ep', axis=0, tiled=True)  21.7 us
    dot_general x2, matrix products, contract_first(): lax.dot_general(left, right, (((0,), (0,)), ((), ())), preferred_element_...  13.8 us
  transfers between devices with their start and end apart: 10, of which 9 were waited for; matrix products, arithmetic and copies ran while one was open for 10% of the time, Pallas kernels for 0%

profile of v1, /device:TPU:0, one launch (start us, length us, event | category | flops | bytes accessed | tf_op | source)
XLA Modules:
  0.0 489.0 jit_solution(6418308995381881234)
XLA Ops:
  9.2 11.8 %collective-permute-done = bf16[128,3072]{1,0:T(8,128)(2,1)S(1)} collective-permute-done((bf16[128,3072]{1,0:T(8,128)(2,1)}, bf16[128,3072]{1,0:T(8,128)(2,1)S(1)}, u32[]{:S(2)}, u32[]{:S(2)}) %collective-permute-start) | collective-permute-done | bytes 786464 | tf_op jit(solution)/shard_map/ppermute | solution.py:15
  21.1 11.4 %collective-permute-done.1 = bf16[128,3072]{1,0:T(8,128)(2,1)S(1)} collective-permute-done((bf16[128,3072]{1,0:T(8,128)(2,1)S(1)}, bf16[128,3072]{1,0:T(8,128)(2,1)S(1)}, u32[]{:S(2)}, u32[]{:S(2)}) %collective-permute-start.1) | collective-permute-done | bytes 786464 | tf_op jit(solution)/shard_map/ppermute | solution.py:15
  33.2 11.5 %all_gather.14 = f32[512,4]{0,1:T(4,128)S(1)} all-gather(f32[128,4]{0,1:T(4,128)S(1)} %select_reduce_fusion.1), channel_id=1, replica_groups=mesh['fsdp'=8,'ep'=4] {'ep'}, dimensions={0}, use_global_device_ids=true | all-gather | bytes 10240 | tf_op jit(solution)/shard_map/all_gather | solution.py:54
  44.8 0.9 constant_dynamic-update-slice_fusion.7
  45.8 1.0 constant_dynamic-update-slice_fusion.6
  46.7 0.9 constant_dynamic-update-slice_fusion.5
  47.7 0.9 constant_dynamic-update-slice_fusion.4
  48.6 0.9 constant_dynamic-update-slice_fusion.3
  49.5 0.9 constant_dynamic-update-slice_fusion.2
  50.5 1.0 constant_dynamic-update-slice_fusion.1
  51.4 0.9 constant_dynamic-update-slice_fusion
  52.4 40.4 %all-gather.4.cloned.1.call-done = bf16[1,3072,768]{2,1,0:T(8,128)(2,1)} async-done(((bf16[1,384,768]{2,1,0:T(8,128)(2,1)}), bf16[1,3072,768]{2,1,0:T(8,128)(2,1)}) %all-gather.4.cloned.1.call-update) | async-done | bytes 4718608 | tf_op jit(solution)/shard_map/all_gather | solution.py:58
  92.8 5.9 %fusion.5 = f32[512,768]{1,0:T(8,128)S(1)} fusion(bf16[1,3072,768]{2,1,0:T(8,128)(2,1)} %all-gather.4.cloned.1.call-done, bf16[1024,3072]{1,0:T(8,128)(2,1)} %constant_dynamic-update-slice_fusion, s32[]{:T(128)S(6)} %select_n.22), kind=kOutput, calls=%fused_computation.9 | convolution fusion | flops 2415919104 | bytes 9437188 | tf_op jit(solution)/shard_map/dot_general | solution.py:62
  98.7 74.3 %all-gather.6.cloned.1.call-done = bf16[1,768,3072]{2,1,0:T(8,128)(2,1)} async-done(((bf16[1,96,3072]{2,1,0:T(8,128)(2,1)}), bf16[1,768,3072]{2,1,0:T(8,128)(2,1)}) %all-gather.6.cloned.1.call-update) | async-done | bytes 4718608 | tf_op jit(solution)/shard_map/all_gather | solution.py:60
  173.0 6.5 %multiply_convert_fusion.1 = bf16[512,3072]{1,0:T(8,128)(2,1)} fusion(bf16[1,768,3072]{2,1,0:T(8,128)(2,1)} %all-gather.6.cloned.1.call-done, f32[512]{0:T(512)S(1)} %select_reduce_fusion, f32[512,768]{1,0:T(8,128)S(1)} %fusion.5), kind=kOutput, calls=%fused_computation.1 | convolution fusion | flops 2422603776 | bytes 9439232 | tf_op jit(solution)/shard_map/dot_general | solution.py:73
  179.6 21.7 %all-gather.8.cloned.1.call-done = bf16[512,3072]{1,0:T(8,128)(2,1)} async-done(((bf16[128,3072]{1,0:T(8,128)(2,1)}), bf16[512,3072]{1,0:T(8,128)(2,1)}) %all-gather.8.cloned.1.call-update) | async-done | bytes 3145744 | tf_op jit(solution)/shard_map/all_gather | solution.py:59
  201.3 6.6 %fusion.18 = bf16[512,768]{1,0:T(8,128)(2,1)S(1)} fusion(f32[512,768]{1,0:T(8,128)S(1)} %fusion.5, bf16[1,768,3072]{2,1,0:T(8,128)(2,1)} %all-gather.6.cloned.1.call-done, bf16[512,3072]{1,0:T(8,128)(2,1)} %all-gather.8.cloned.1.call-done, f32[512]{0:T(512)S(1)} %select_reduce_fusion), kind=kOutput, calls=%fused_computation.22 | convolution fusion | flops 2428108800 | bytes 10225664 | tf_op jit(solution)/shard_map/dot_general | solution.py:37
  207.9 6.9 %fusion.7 = bf16[512,3072]{1,0:T(8,128)(2,1)} fusion(bf16[512,768]{1,0:T(8,128)(2,1)S(1)} %fusion.18, bf16[1,3072,768]{2,1,0:T(8,128)(2,1)} %all-gather.4.cloned.1.call-done), kind=kOutput, calls=%fused_computation.11 | convolution fusion | flops 2417491968 | bytes 8650752 | tf_op jit(solution)/shard_map/dot_general | solution.py:37
  214.9 6.8 %convolution_convert_fusion.1 = bf16[3072,768]{1,0:T(8,128)(2,1)} fusion(bf16[512,768]{1,0:T(8,128)(2,1)S(1)} %fusion.18, bf16[1024,3072]{1,0:T(8,128)(2,1)} %constant_dynamic-update-slice_fusion, s32[]{:T(128)S(6)} %select_n.22), kind=kOutput, calls=%fused_computation.3 | convolution fusion | flops 2418278400 | bytes 8650756 | tf_op jit(solution)/shard_map/dot_general | solution.py:43
  221.7 7.0 %convolution_convert_fusion = bf16[768,3072]{1,0:T(8,128)(2,1)} fusion(bf16[512,3072]{1,0:T(8,128)(2,1)} %all-gather.8.cloned.1.call-done, f32[512]{0:T(512)S(1)} %select_reduce_fusion, f32[512,768]{1,0:T(8,128)S(1)} %fusion.5), kind=kOutput, calls=%fused_computation.2 | convolution fusion | flops 2426535936 | bytes 9439232 | tf_op jit(solution)/shard_map/dot_general | solution.py:43
  228.7 13.5 %reduce-scatter.5.cloned.1.call-done = bf16[128,3072]{1,0:T(8,128)(2,1)} async-done(((bf16[512,3072]{1,0:T(8,128)(2,1)}), bf16[128,3072]{1,0:T(8,128)(2,1)}) %reduce-scatter.5.cloned.1.call-update) | async-done | bytes 786448 | tf_op jit(solution)/shard_map/reduce_scatter | solution.py:74
  242.3 41.1 %reduce-scatter.7.cloned.1.call-done = bf16[128,3072]{1,0:T(8,128)(2,1)} async-done(((bf16[512,3072]{1,0:T(8,128)(2,1)}), bf16[128,3072]{1,0:T(8,128)(2,1)}) %reduce-scatter.7.cloned.1.call-update) | async-done | bytes 786448 | tf_op jit(solution)/shard_map/reduce_scatter | solution.py:76
  283.4 99.5 %reduce-scatter.9.cloned.1.call-done = bf16[384,768]{1,0:T(8,128)(2,1)} async-done(((bf16[3072,768]{1,0:T(8,128)(2,1)}), bf16[384,768]{1,0:T(8,128)(2,1)}) %reduce-scatter.9.cloned.1.call-update) | async-done | bytes 589840 | tf_op jit(solution)/shard_map/reduce_scatter | solution.py:70
  382.9 99.3 %reduce-scatter.11.cloned.1.call-done = bf16[96,3072]{1,0:T(8,128)(2,1)} async-done(((bf16[768,3072]{1,0:T(8,128)(2,1)}), bf16[96,3072]{1,0:T(8,128)(2,1)}) %reduce-scatter.11.cloned.1.call-update) | async-done | bytes 589840 | tf_op jit(solution)/shard_map/reduce_scatter | solution.py:65
  (23 shorter events, 3.1 us)
Async XLA Ops:
  7.2 85.6 %all-gather.4.cloned.1.call-start = ((), (), s32[]{:S(2)}) async-start(), calls=%async_computation.4 | async-start | bytes 5308416 | tf_op jit(solution)/shard_map/all_gather | solution.py:58
  7.9 39.8 %copy-start = (bf16[128,3072]{1,0:T(8,128)(2,1)S(1)}, bf16[128,3072]{1,0:T(8,128)(2,1)}, u32[]{:S(2)}) copy-start(bf16[128,3072]{1,0:T(8,128)(2,1)} %param.6) | copy-start | bytes 2359300
  7.9 165.1 %all-gather.6.cloned.1.call-start = ((), (), s32[]{:S(2)}) async-start(), calls=%async_computation.5 | async-start | bytes 5308416 | tf_op jit(solution)/shard_map/all_gather | solution.py:60
  8.7 192.6 %all-gather.8.cloned.1.call-start = ((), (), s32[]{:S(2)}) async-start(), calls=%async_computation.7 | async-start | bytes 3932160 | tf_op jit(solution)/shard_map/all_gather | solution.py:59
  8.7 12.3 %collective-permute-start = (bf16[128,3072]{1,0:T(8,128)(2,1)}, bf16[128,3072]{1,0:T(8,128)(2,1)S(1)}, u32[]{:S(2)}, u32[]{:S(2)}) collective-permute-start(bf16[128,3072]{1,0:T(8,128)(2,1)} %param.6), channel_id=1, source_target_pairs={{0,1},{1,2},{2,3},{3,0},{4,5},{5,6},{6,7},{7,4},{8,9},{9,10},{10,1... | collective-permute-start | bytes 2359304 | tf_op jit(solution)/shard_map/ppermute | solution.py:15
  21.0 11.4 %collective-permute-start.1 = (bf16[128,3072]{1,0:T(8,128)(2,1)S(1)}, bf16[128,3072]{1,0:T(8,128)(2,1)S(1)}, u32[]{:S(2)}, u32[]{:S(2)}) collective-permute-start(bf16[128,3072]{1,0:T(8,128)(2,1)S(1)} %collective-permute-done), channel_id=1, source_target_pairs={{0,1},{1,2},{2,3},{3,0},{4,5},{5,6},{6,7},{7,4},{8,9},{9,10},{10,1... | collective-permute-start | bytes 2359304 | tf_op jit(solution)/shard_map/ppermute | solution.py:15
  32.4 12.4 %collective-permute-start.2 = (bf16[128,3072]{1,0:T(8,128)(2,1)S(1)}, bf16[128,3072]{1,0:T(8,128)(2,1)S(1)}, u32[]{:S(2)}, u32[]{:S(2)}) collective-permute-start(bf16[128,3072]{1,0:T(8,128)(2,1)S(1)} %collective-permute-done.1), channel_id=1, source_target_pairs={{0,1},{1,2},{2,3},{3,0},{4,5},{5,6},{6,7},{7,4},{8,9},{9,10},{10,1... | collective-permute-start | bytes 2359304 | tf_op jit(solution)/shard_map/ppermute | solution.py:15
  32.5 209.8 %reduce-scatter.5.cloned.1.call-start = ((), (), s32[]{:S(2)}) async-start(), calls=%async_computation.6 | async-start | bytes 3932160 | tf_op jit(solution)/shard_map/reduce_scatter | solution.py:74
  179.5 103.9 %reduce-scatter.7.cloned.1.call-start = ((), (), s32[]{:S(2)}) async-start(), calls=%async_computation.8 | async-start | bytes 3932160 | tf_op jit(solution)/shard_map/reduce_scatter | solution.py:76
  214.8 168.1 %reduce-scatter.9.cloned.1.call-start = ((), (), s32[]{:S(2)}) async-start(), calls=%async_computation.9 | async-start | bytes 5308416 | tf_op jit(solution)/shard_map/reduce_scatter | solution.py:70
  221.7 260.5 %reduce-scatter.11.cloned.1.call-start = ((), (), s32[]{:S(2)}) async-start(), calls=%async_computation.10 | async-start | bytes 5308416 | tf_op jit(solution)/shard_map/reduce_scatter | solution.py:65
Sparse Core Ops, SparseCore 0:
  10.2 82.5 all-gather.3
  95.0 78.0 all-gather.5
  174.6 26.6 all-gather.7
  204.3 37.9 reduce-scatter.4
  245.4 37.9 reduce-scatter.6
  287.5 95.4 reduce-scatter.8
  387.1 94.9 reduce-scatter.10
